TPU v7x, 256 devices: a whole 4x4x8 slice. The times are simulated.
256 devices in a mesh: leaf: 16 (over x, y), blk: 16 (over z, core).
Axes of the slice: x: 4, y: 4, z: 8, core: 2. Of those that a mesh axis runs over, the one named last changes fastest.
Arguments:
- near_tiles: bfloat16 [128, 16, 512, 512], P('leaf', 'blk'), may hold values from -0.25 to 0.25
- near_cols: int32 [128, 16], P('leaf', 'blk'), may hold values from 0 to 127, as said below
- near_count: int32 [128], P('leaf'), may hold values from 1 to 16, as said below
- probes: bfloat16 [128, 512, 512], P('leaf'), may hold values from -6 to 6
- mixing: float32 [512, 64], replicated, may hold values from -0.25 to 0.25
- far_tiles: bfloat16 [128, 16, 512, 512], P('leaf', 'blk'), may hold values from -6 to 6
- far_cols: int32 [128, 16], P('leaf', 'blk'), may hold values from 0 to 127, as said below
Outputs:
- coupling: float32 [128, 16, 64, 64], P('leaf', 'blk')
- root_part: float32 [128, 64, 64], P('leaf')
Inputs may be any that keep to these rules, and one draw needn't show every extreme that they name: near_cols[r, k] lies within 8 of r; the slots below near_count[r] name distinct clusters. Slots at or past near_count[r] hold arbitrary tiles that must be ignored. far_cols[r, j] differs from r by more than 8.
All inputs are finite; a program needn't handle non-finite values.
Results may differ from a plain program's by a relative error of at most 0.0041.
Values may be sent and summed in bfloat16 or wider, within the bound.
No kernel may reach another device: no remote copies, remote signals or barrier semaphores. Data moves between devices by JAX's collectives and lax.ppermute only.
A program may use at most 128 MiB of HBM per device.

v0:
```python
import math
import jax
import jax.numpy as jnp
from jax import lax
from jax.sharding import PartitionSpec as P

RANK = 64
REACH = 8
highest = lax.Precision.HIGHEST


def padded(value, sides, width):
    for axis, dim in sides:
        peers, length = (lax.axis_size(axis), value.shape[dim])
        up = [(i, (i + 1) % peers) for i in range(peers - 1)]
        down = [(j, i) for i, j in up]
        last = lax.slice_in_dim(value, length - width, length, axis=dim)
        leading = lax.slice_in_dim(value, 0, width, axis=dim)
        before = lax.ppermute(last, axis, up)
        after = lax.ppermute(leading, axis, down)
        value = jnp.concatenate([before, value, after], axis=dim)
    return value


def partner_2(block, axis, apart):
    count = lax.axis_size(axis)
    route = []
    for low in range(count):
        high = low | 1 << apart
        if high != low and high < count:
            route += [(low, high), (high, low)]
    return lax.ppermute(block, axis, route)


def basis_from(gram_matrix, mixed_rows):
    lower_factor = jnp.linalg.cholesky(gram_matrix)
    solved = jax.scipy.linalg.solve_triangular(
        lower_factor, jnp.swapaxes(mixed_rows, -1, -2), lower=True
    )
    return jnp.swapaxes(solved, -1, -2)


def merge(stacked, mixing):
    mixed_rows = jnp.einsum("...mp,pk->...mk", stacked, mixing, precision=highest)
    gram_matrix = jnp.einsum("...mk,...ml->...kl", mixed_rows, mixed_rows, precision=highest)
    transfer = basis_from(gram_matrix, mixed_rows)
    merged = jnp.einsum("...mk,...mp->...kp", transfer, stacked, precision=highest)
    return (transfer, merged)


def shards(near_tiles, near_cols, near_count, probes, mixing, far_tiles, far_cols):
    local_rows = probes.shape[0]
    near_dev = near_tiles.shape[1]
    leaf_pos = lax.axis_index("leaf")
    blk_pos = lax.axis_index("blk")
    subtrees = lax.axis_size("leaf")
    clusters = local_rows * subtrees
    first_cluster = leaf_pos * local_rows - REACH
    window = padded(probes, (("leaf", 0),), REACH)

    def leaf_sketch(row_index):
        running = jnp.zeros((probes.shape[1], probes.shape[2]), jnp.float32)
        column = near_cols[row_index, 0] - first_cluster
        probe_block = lax.dynamic_index_in_dim(window, column, 0, keepdims=False)
        near_tile = near_tiles[row_index, 0]
        is_live = blk_pos * near_dev + 0 < near_count[row_index]
        running = lax.cond(
            is_live,
            lambda current: jnp.dot(near_tile, probe_block, preferred_element_type=jnp.float32),
            lambda current: current,
            running,
        )
        return running

    partial_sketch = lax.map(leaf_sketch, jnp.arange(local_rows))
    sketch_rows = lax.psum_scatter(partial_sketch, "blk", scatter_dimension=1, tiled=True)
    mixed_rows = jnp.einsum("rbp,pk->rbk", sketch_rows, mixing, precision=highest)
    gram_part = jnp.einsum("rbk,rbl->rkl", mixed_rows, mixed_rows, precision=highest)
    gram_matrix = lax.psum(gram_part, "blk")
    basis_part = basis_from(gram_matrix, mixed_rows)
    proj_part = jnp.einsum("rbk,rbp->rkp", basis_part, sketch_rows, precision=highest)
    leaf_proj = lax.psum(proj_part, "blk")
    basis_low = lax.all_gather(basis_part.astype(jnp.bfloat16), "blk", axis=1, tiled=True)
    all_bases = lax.all_gather(basis_low, "leaf", axis=0, tiled=True)
    far_basis = all_bases[far_cols]
    far_image = jnp.einsum(
        "rjab,rjbk->rjak", far_tiles, far_basis, preferred_element_type=jnp.float32
    )
    coupling = jnp.einsum(
        "rak,rjal->rjkl", basis_low.astype(jnp.float32), far_image, precision=highest
    )
    sub_stack = leaf_proj.reshape(local_rows * RANK, leaf_proj.shape[2])
    sub_transfer, node_sketch = merge(sub_stack, mixing)
    levels = subtrees.bit_length() - 1
    path_factor = jnp.eye(RANK, dtype=jnp.float32)
    for depth_index in range(levels):
        partner = partner_2(node_sketch.astype(jnp.bfloat16), "leaf", depth_index).astype(
            node_sketch.dtype
        )
        is_upper = leaf_pos >> depth_index & 1
        lower_half = jnp.where(is_upper == 1, partner, node_sketch)
        upper_half = jnp.where(is_upper == 1, node_sketch, partner)
        transfer, node_sketch = merge(jnp.concatenate([lower_half, upper_half], 0), mixing)
        picked = lax.dynamic_slice_in_dim(transfer, is_upper * RANK, RANK, 0)
        path_factor = jnp.dot(path_factor, picked, precision=highest)
    sub_blocks = sub_transfer.reshape(local_rows, RANK, RANK)
    root_part = jnp.einsum("cab,bd->cad", sub_blocks, path_factor, precision=highest)
    root_part = root_part * math.sqrt(clusters * RANK)
    return (coupling, root_part)


def solution(mesh):
    in_specs = (
        P("leaf", "blk", None, None),
        P("leaf", "blk"),
        P("leaf"),
        P("leaf", None, None),
        P(),
        P("leaf", "blk", None, None),
        P("leaf", "blk"),
    )
    out_specs = (P("leaf", "blk", None, None), P("leaf", None, None))
    return jax.shard_map(shards, mesh=mesh, in_specs=in_specs, out_specs=out_specs, check_vma=False)
```

profile of v0, /device:TPU:22, one launch (start us, length us, event | category | flops | bytes accessed | tf_op | source)
XLA Modules:
  0.0 679.8 jit_solution(7134080984132930772)
XLA Ops:
  7.2 3.2 collective-permute-start
  10.4 2.7 collective-permute-start.1
  13.1 88.6 %collective-permute-done = bf16[8,512,512]{2,1,0:T(8,128)(2,1)} collective-permute-done((bf16[8,512,512]{2,1,0:T(8,128)(2,1)}, bf16[8,512,512]{2,1,0:T(8,128)(2,1)}, u32[]{:S(2)}, u32[]{:S(2)}) %collective-permute-start) | collective-permute-done | bytes 4194336 | tf_op jit(solution)/shard_map/ppermute | solution.py:19
  101.7 2.9 collective-permute-done.1
  104.7 10.8 %pad_maximum_fusion = bf16[24,512,512]{2,1,0:T(8,128)(2,1)} fusion(bf16[8,512,512]{2,1,0:T(8,128)(2,1)} %collective-permute-done.1, bf16[8,512,512]{2,1,0:T(8,128)(2,1)} %param.17, bf16[8,512,512]{2,1,0:T(8,128)(2,1)} %collective-permute-done), kind=kLoop, calls=%fused_computation.9 | loop fusion | flops 12582912 | bytes 25165824 | tf_op jit(solution)/shard_map/concatenate | solution.py:21
  115.4 60.4 %while.10 = (s32[]{:T(128)}, f32[8,512,512]{2,1,0:T(8,128)}, s32[8]{0:T(128)S(1)}, s32[8]{0:T(128)S(1)}, s32[]{:T(128)}, /*index=5*/bf16[8,1,512,512]{3,2,1,0:T(...) while((s32[]{:T(128)}, f32[8,512,512]{2,1,0:T(8,128)}, ...), condition=%wide.region_3.4_spmd, body=%wide.region_0.3_spmd.sunk | while | flops 268435456 | bytes 4195627 | solution.py:75
  119.1 2.8 conditional.2
  120.3 1.6 convolution_bitcast_fusion
  126.7 2.8 conditional.2
  127.9 1.6 convolution_bitcast_fusion
  134.2 2.8 conditional.2
  135.4 1.6 convolution_bitcast_fusion
  141.7 2.8 conditional.2
  142.9 1.6 convolution_bitcast_fusion
  149.3 2.8 conditional.2
  150.4 1.6 convolution_bitcast_fusion
  156.8 2.8 conditional.2
  158.0 1.6 convolution_bitcast_fusion
  164.4 2.8 conditional.2
  165.6 1.6 convolution_bitcast_fusion
  171.9 2.8 conditional.2
  173.1 1.6 convolution_bitcast_fusion
  175.9 75.0 %reduce-scatter.2.cloned.1.call-done = f32[8,32,512]{2,1,0:T(8,128)} async-done(((f32[8,512,512]{2,1,0:T(8,128)}), f32[8,32,512]{2,1,0:T(8,128)}) %reduce-scatter.2.cloned.1.call-update) | async-done | bytes 524304 | tf_op jit(solution)/shard_map/reduce_scatter | solution.py:76
  250.8 1.6 fusion.20
  253.9 108.8 %all-reduce.3.cloned.1.call-done = f32[8,64,64]{1,2,0:T(8,128)} async-done(((f32[8,64,64]{1,2,0:T(8,128)}), f32[8,64,64]{1,2,0:T(8,128)}) %all-reduce.3.cloned.1.call-update) | async-done | bytes 131088 | tf_op jit(solution)/shard_map/psum | solution.py:79
  364.8 46.9 %custom-call.17 = f32[8,64,64]{2,1,0:T(8,128)S(1)} custom-call(f32[8,64,64]{2,1,0:T(8,128)S(1)} %fusion.13), custom_call_target="Cholesky" | custom-call | tf_op jit(solution)/shard_map/jit(cholesky)/cholesky | solution.py:36
  411.9 39.3 %custom-call.18 = f32[8,1,64,64]{2,3,1,0:T(8,128)S(1)} custom-call(f32[8,1,64,64]{3,2,1,0:T(8,128)S(1)} %select_bitcast_fusion), custom_call_target="InvertDiagBlocksLowerTriangular" | custom-call | tf_op jit(solution)/shard_map/jit(_solve_triangular)/vmap()/triangular_solve | solution.py:37
  451.6 3.1 fusion.70
  454.9 18.4 %all_gather.6 = bf16[8,512,64]{2,1,0:T(8,128)(2,1)S(1)} all-gather(bf16[8,32,64]{2,1,0:T(8,128)(2,1)S(1)} %convert_bitcast_fusion), channel_id=1, replica_groups=mesh['leaf'=16,'blk'=16] {'blk'}, dimensions={1}, use_global_device_ids=true | all-gather | bytes 557056 | tf_op jit(solution)/shard_map/all_gather | solution.py:83
  474.5 93.2 %all-reduce.5.cloned.1.call-done = f32[512,512]{1,0:T(8,128)} async-done(((f32[512,512]{1,0:T(8,128)}), f32[512,512]{1,0:T(8,128)}) %all-reduce.5.cloned.1.call-update) | async-done | bytes 1048592 | tf_op jit(solution)/shard_map/psum | solution.py:82
  567.8 2.4 fusion.71
  570.5 5.8 cholesky.127
  577.7 4.9 custom-call.19
  582.9 2.0 fusion.65
  586.5 4.7 collective-permute-done.2
  591.9 5.8 cholesky.138
  599.1 4.9 custom-call.23
  605.3 5.9 collective-permute-done.3
  611.9 5.8 cholesky.149
  619.1 4.9 custom-call.24
  625.4 5.0 collective-permute-done.4
  631.1 5.8 cholesky.160
  638.3 4.9 custom-call.25
  645.6 4.3 collective-permute-done.5
  650.5 5.8 cholesky.171
  657.7 4.9 custom-call.26
  664.2 4.0 gather_fusion
  668.2 3.6 fusion.5
  (122 shorter events, 47.9 us)
Async XLA Ops:
  7.2 243.7 %copy-start = (f32[512,64]{0,1:T(8,128)S(1)}, f32[512,64]{0,1:T(8,128)}, u32[]{:S(2)}) copy-start(f32[512,64]{0,1:T(8,128)} %param.18) | copy-start | bytes 393220
  7.2 243.7 %reduce-scatter.2.cloned.1.call-start = ((), (), s32[]{:S(2)}) async-start(), calls=%async_computation.1 | async-start | bytes 8912896 | tf_op jit(solution)/shard_map/reduce_scatter | solution.py:76
  7.2 94.5 %collective-permute-start = (bf16[8,512,512]{2,1,0:T(8,128)(2,1)}, bf16[8,512,512]{2,1,0:T(8,128)(2,1)}, u32[]{:S(2)}, u32[]{:S(2)}) collective-permute-start(bf16[8,512,512]{2,1,0:T(8,128)(2,1)} %param.17), channel_id=1, source_target_pairs={{0,16},{16,32},{32,48},{48,64},{64,80},{80,96},{96,112},{112,128},... | collective-permute-start | bytes 12582920 | tf_op jit(solution)/shard_map/ppermute | solution.py:19
  10.4 94.2 %collective-permute-start.1 = (bf16[8,512,512]{2,1,0:T(8,128)(2,1)}, bf16[8,512,512]{2,1,0:T(8,128)(2,1)}, u32[]{:S(2)}, u32[]{:S(2)}) collective-permute-start(bf16[8,512,512]{2,1,0:T(8,128)(2,1)} %param.17), channel_id=1, source_target_pairs={{16,0},{32,16},{48,32},{64,48},{80,64},{96,80},{112,96},{128,112},... | collective-permute-start | bytes 12582920 | tf_op jit(solution)/shard_map/ppermute | solution.py:20
  13.1 102.3 %copy-start.1 = (s32[8]{0:T(128)S(1)}, s32[8]{0:T(128)}, u32[]{:S(2)}) copy-start(s32[8]{0:T(128)} %param.16) | copy-start | bytes 100
  13.1 102.3 %copy-start.2 = (s32[8,1]{0,1:T(1,128)S(1)}, s32[8,1]{0,1:T(1,128)}, u32[]{:S(2)}) copy-start(s32[8,1]{0,1:T(1,128)} %param.15) | copy-start | bytes 100
  175.8 298.7 %copy-start.3 = (s32[8,1]{0,1:T(1,128)S(1)}, s32[8,1]{0,1:T(1,128)}, u32[]{:S(2)}) copy-start(s32[8,1]{0,1:T(1,128)} %param.20) | copy-start | bytes 100
  175.8 186.9 %all-reduce.3.cloned.1.call-start = ((), (), s32[]{:S(2)}) async-start(), calls=%async_computation.2 | async-start | bytes 524288 | tf_op jit(solution)/shard_map/psum | solution.py:79
  253.8 314.0 %all-reduce.5.cloned.1.call-start = ((), (), s32[]{:S(2)}) async-start(), calls=%async_computation.4 | async-start | bytes 2097152 | tf_op jit(solution)/shard_map/psum | solution.py:82
  454.8 209.4 %all-gather.2.cloned.1.call-start = ((), (), s32[]{:S(2)}) async-start(), calls=%async_computation.3 | async-start | bytes 8912896 | tf_op jit(solution)/shard_map/all_gather | solution.py:84
  584.9 6.3 collective-permute-start.2
  604.5 6.7 collective-permute-start.3
  624.5 5.9 collective-permute-start.4
  643.7 6.1 collective-permute-start.5
Sparse Core Ops, SparseCore 0:
  175.9 74.8 reduce-scatter.1
  253.9 108.7 all-reduce.2
  454.9 112.7 all-reduce.4
  570.0 76.4 all-gather.1
where the time goes:
time: 681 us; the launch traced here: 680 us
  waiting for transfers between devices  388 us (57%)
  other arithmetic  159 us (23%)
  matrix products  35 us (5%)
  local copies, waits for them, and re-layouts  30.2 us (4%)
  loops' own time  24.6 us (4%)
  blocking collectives  18.4 us (3%)
  between operations  14.2 us (2%)
  starting transfers between devices  10.2 us (1%)
    psum x1, waiting for transfers between devices, shards(): gram_matrix = lax.psum(gram_part, 'blk')  109 us
    psum x1, waiting for transfers between devices, shards(): leaf_proj = lax.psum(proj_part, 'blk')  93.2 us
    ppermute x1, waiting for transfers between devices, padded(): before = lax.ppermute(last, axis, up)  88.6 us
    another operation x19, other arithmetic, basis_from(): lower_factor = jnp.linalg.cholesky(gram_matrix)  79.7 us
    reduce_scatter x1, waiting for transfers between devices, shards(): lax.psum_scatter(partial_sketch, 'blk', scatter_dimension=1, tiled=True)  75 us
    another operation x13, other arithmetic, basis_from(): jax.scipy.linalg.solve_triangular(lower_factor, jnp.swapaxes(mixed_rows,...  67.2 us
    another operation x1, loops' own time, shards(): partial_sketch = lax.map(leaf_sketch, jnp.arange(local_rows))  19.8 us
    ppermute x4, waiting for transfers between devices, partner_2(): return lax.ppermute(block, axis, route)  19.7 us
  transfers between devices with their start and end apart: 10, of which 9 were waited for; matrix products, arithmetic and copies ran while one was open for 11% of the time, Pallas kernels for 0%

commit v1 on v0

--- a/solution.py
+++ b/solution.py
@@ -79,7 +79,7 @@
     gram_matrix = lax.psum(gram_part, "blk")
     basis_part = basis_from(gram_matrix, mixed_rows)
     proj_part = jnp.einsum("rbk,rbp->rkp", basis_part, sketch_rows, precision=highest)
-    leaf_proj = lax.psum(proj_part, "blk")
+    leaf_proj = jnp.sum(lax.all_gather(proj_part, "blk"), axis=0)
     basis_low = lax.all_gather(basis_part.astype(jnp.bfloat16), "blk", axis=1, tiled=True)
     all_bases = lax.all_gather(basis_low, "leaf", axis=0, tiled=True)
     far_basis = all_bases[far_cols]

time: 681 us -> 752 us (1.10)
  waiting for transfers between devices: 388 us -> 451 us
  other arithmetic: 159 us -> 167 us
    psum x1 -> x0, waiting for transfers between devices: 93.2 us -> none  [shards(): leaf_proj = lax.psum(proj_part, 'blk')]
    all_gather x0 -> x1, waiting for transfers between devices: none -> 90.8 us  [shards(): leaf_proj = jnp.sum(lax.all_gather(proj_part, 'blk'), axis=0)]
    all_gather x1, waiting for transfers between devices: 0.01 us -> 71.2 us  [shards(): all_bases = lax.all_gather(basis_low, 'leaf', axis=0, tiled=True)]
    reduce_sum x0 -> x1, other arithmetic: none -> 7.93 us  [shards(): leaf_proj = jnp.sum(lax.all_gather(proj_part, 'blk'), axis=0)]
  transfers between devices with their start and end apart: 10 -> 10, of which waited for: 9 -> 10; matrix products, arithmetic and copies ran while one was open for 11% -> 2% of each run, Pallas kernels for 0% -> 0%
where the time goes in v1:
time: 752 us; the launch traced here: 750 us
  waiting for transfers between devices  451 us (60%)
  other arithmetic  167 us (22%)
  matrix products  33.8 us (4%)
  local copies, waits for them, and re-layouts  30.2 us (4%)
  loops' own time  24.6 us (3%)
  blocking collectives  18.4 us (2%)
  between operations  14.2 us (2%)
  starting transfers between devices  10.7 us (1%)
    psum x1, waiting for transfers between devices, shards(): gram_matrix = lax.psum(gram_part, 'blk')  109 us
    all_gather x1, waiting for transfers between devices, shards(): leaf_proj = jnp.sum(lax.all_gather(proj_part, 'blk'), axis=0)  90.8 us
    ppermute x1, waiting for transfers between devices, padded(): before = lax.ppermute(last, axis, up)  88.6 us
    another operation x19, other arithmetic, basis_from(): lower_factor = jnp.linalg.cholesky(gram_matrix)  79.7 us
    reduce_scatter x1, waiting for transfers between devices, shards(): lax.psum_scatter(partial_sketch, 'blk', scatter_dimension=1, tiled=True)  75 us
    all_gather x1, waiting for transfers between devices, shards(): all_bases = lax.all_gather(basis_low, 'leaf', axis=0, tiled=True)  71.2 us
    another operation x13, other arithmetic, basis_from(): jax.scipy.linalg.solve_triangular(lower_factor, jnp.swapaxes(mixed_rows,...  67.8 us
    another operation x1, loops' own time, shards(): partial_sketch = lax.map(leaf_sketch, jnp.arange(local_rows))  19.8 us
  transfers between devices with their start and end apart: 10, of which 10 were waited for; matrix products, arithmetic and copies ran while one was open for 2% of the time, Pallas kernels for 0%

profile of v1, /device:TPU:22, one launch (start us, length us, event | category | flops | bytes accessed | tf_op | source)
XLA Modules:
  0.0 750.5 jit_solution(17221751738433635304)
XLA Ops:
  7.2 3.2 collective-permute-start
  10.4 2.7 collective-permute-start.1
  13.1 88.6 %collective-permute-done = bf16[8,512,512]{2,1,0:T(8,128)(2,1)} collective-permute-done((bf16[8,512,512]{2,1,0:T(8,128)(2,1)}, bf16[8,512,512]{2,1,0:T(8,128)(2,1)}, u32[]{:S(2)}, u32[]{:S(2)}) %collective-permute-start) | collective-permute-done | bytes 4194336 | tf_op jit(solution)/shard_map/ppermute | solution.py:19
  101.7 2.9 collective-permute-done.1
  104.7 10.8 %pad_maximum_fusion = bf16[24,512,512]{2,1,0:T(8,128)(2,1)} fusion(bf16[8,512,512]{2,1,0:T(8,128)(2,1)} %collective-permute-done.1, bf16[8,512,512]{2,1,0:T(8,128)(2,1)} %param.17, bf16[8,512,512]{2,1,0:T(8,128)(2,1)} %collective-permute-done), kind=kLoop, calls=%fused_computation.9 | loop fusion | flops 12582912 | bytes 25165824 | tf_op jit(solution)/shard_map/concatenate | solution.py:21
  115.4 60.4 %while.10 = (s32[]{:T(128)}, f32[8,512,512]{2,1,0:T(8,128)}, s32[8]{0:T(128)S(1)}, s32[8]{0:T(128)S(1)}, s32[]{:T(128)}, /*index=5*/bf16[8,1,512,512]{3,2,1,0:T(...) while((s32[]{:T(128)}, f32[8,512,512]{2,1,0:T(8,128)}, ...), condition=%wide.region_3.4_spmd, body=%wide.region_0.3_spmd.sunk | while | flops 268435456 | bytes 4195627 | solution.py:75
  119.1 2.8 conditional.2
  120.3 1.6 convolution_bitcast_fusion
  126.7 2.8 conditional.2
  127.9 1.6 convolution_bitcast_fusion
  134.2 2.8 conditional.2
  135.4 1.6 convolution_bitcast_fusion
  141.7 2.8 conditional.2
  142.9 1.6 convolution_bitcast_fusion
  149.3 2.8 conditional.2
  150.4 1.6 convolution_bitcast_fusion
  156.8 2.8 conditional.2
  158.0 1.6 convolution_bitcast_fusion
  164.4 2.8 conditional.2
  165.6 1.6 convolution_bitcast_fusion
  171.9 2.8 conditional.2
  173.1 1.6 convolution_bitcast_fusion
  175.9 75.0 %reduce-scatter.2.cloned.1.call-done = f32[8,32,512]{2,1,0:T(8,128)} async-done(((f32[8,512,512]{2,1,0:T(8,128)}), f32[8,32,512]{2,1,0:T(8,128)}) %reduce-scatter.2.cloned.1.call-update) | async-done | bytes 524304 | tf_op jit(solution)/shard_map/reduce_scatter | solution.py:76
  250.8 1.6 fusion.20
  253.9 108.8 %all-reduce.2.cloned.1.call-done = f32[8,64,64]{1,2,0:T(8,128)} async-done(((f32[8,64,64]{1,2,0:T(8,128)}), f32[8,64,64]{1,2,0:T(8,128)}) %all-reduce.2.cloned.1.call-update) | async-done | bytes 131088 | tf_op jit(solution)/shard_map/psum | solution.py:79
  364.8 46.9 %custom-call.17 = f32[8,64,64]{2,1,0:T(8,128)S(1)} custom-call(f32[8,64,64]{2,1,0:T(8,128)S(1)} %fusion.13), custom_call_target="Cholesky" | custom-call | tf_op jit(solution)/shard_map/jit(cholesky)/cholesky | solution.py:36
  411.9 39.3 %custom-call.18 = f32[8,1,64,64]{2,3,1,0:T(8,128)S(1)} custom-call(f32[8,1,64,64]{3,2,1,0:T(8,128)S(1)} %select_bitcast_fusion), custom_call_target="InvertDiagBlocksLowerTriangular" | custom-call | tf_op jit(solution)/shard_map/jit(_solve_triangular)/vmap()/triangular_solve | solution.py:37
  451.7 18.4 %all_gather.12 = bf16[8,512,64]{2,1,0:T(8,128)(2,1)S(1)} all-gather(bf16[8,32,64]{2,1,0:T(8,128)(2,1)S(1)} %convert_bitcast_fusion), channel_id=1, replica_groups=mesh['leaf'=16,'blk'=16] {'blk'}, dimensions={1}, use_global_device_ids=true | all-gather | bytes 557056 | tf_op jit(solution)/shard_map/all_gather | solution.py:83
  471.4 3.1 fusion.70
  474.6 71.2 %all-gather.4.cloned.1.call-done = bf16[128,512,64]{1,2,0:T(8,128)(2,1)} async-done(((bf16[8,512,64]{1,2,0:T(8,128)(2,1)}), bf16[128,512,64]{1,2,0:T(8,128)(2,1)}) %all-gather.4.cloned.1.call-update) | async-done | bytes 8388624 | tf_op jit(solution)/shard_map/all_gather | solution.py:84
  545.8 4.0 gather_fusion
  549.8 3.6 fusion.5
  553.3 90.8 %all-gather.6.cloned.1.call-done = f32[128,64,512]{2,1,0:T(8,128)} async-done(((f32[8,64,512]{2,1,0:T(8,128)}), f32[128,64,512]{2,1,0:T(8,128)}) %all-gather.6.cloned.1.call-update) | async-done | bytes 16777232 | tf_op jit(solution)/shard_map/all_gather | solution.py:82
  644.1 7.9 %reduce_sum.9 = f32[8,64,512]{2,1,0:T(8,128)S(1)} reduce(f32[16,8,64,512]{3,2,1,0:T(8,128)} %bitcast.137, f32[]{:T(128)} %constant.126.clone.1), dimensions={0}, to_apply=%region_8.9 | reduce | flops 3932160 | bytes 17825796 | tf_op jit(solution)/shard_map/reduce_sum | solution.py:82
  653.6 5.8 cholesky.127
  660.8 5.5 custom-call.19
  671.6 1.7 collective-permute-done.2
  674.0 5.8 cholesky.138
  681.1 4.9 custom-call.23
  687.6 5.0 collective-permute-done.3
  693.4 5.8 cholesky.149
  700.6 4.9 custom-call.24
  707.2 3.2 collective-permute-done.4
  711.1 5.8 cholesky.160
  718.2 4.9 custom-call.25
  725.5 4.1 collective-permute-done.5
  730.2 5.8 cholesky.171
  737.4 4.9 custom-call.26
  (123 shorter events, 51.6 us)
Async XLA Ops:
  7.2 243.7 %copy-start = (f32[512,64]{0,1:T(8,128)S(1)}, f32[512,64]{0,1:T(8,128)}, u32[]{:S(2)}) copy-start(f32[512,64]{0,1:T(8,128)} %param.18) | copy-start | bytes 393220
  7.2 243.7 %reduce-scatter.2.cloned.1.call-start = ((), (), s32[]{:S(2)}) async-start(), calls=%async_computation.1 | async-start | bytes 8912896 | tf_op jit(solution)/shard_map/reduce_scatter | solution.py:76
  7.2 94.5 %collective-permute-start = (bf16[8,512,512]{2,1,0:T(8,128)(2,1)}, bf16[8,512,512]{2,1,0:T(8,128)(2,1)}, u32[]{:S(2)}, u32[]{:S(2)}) collective-permute-start(bf16[8,512,512]{2,1,0:T(8,128)(2,1)} %param.17), channel_id=1, source_target_pairs={{0,16},{16,32},{32,48},{48,64},{64,80},{80,96},{96,112},{112,128},... | collective-permute-start | bytes 12582920 | tf_op jit(solution)/shard_map/ppermute | solution.py:19
  10.4 94.2 %collective-permute-start.1 = (bf16[8,512,512]{2,1,0:T(8,128)(2,1)}, bf16[8,512,512]{2,1,0:T(8,128)(2,1)}, u32[]{:S(2)}, u32[]{:S(2)}) collective-permute-start(bf16[8,512,512]{2,1,0:T(8,128)(2,1)} %param.17), channel_id=1, source_target_pairs={{16,0},{32,16},{48,32},{64,48},{80,64},{96,80},{112,96},{128,112},... | collective-permute-start | bytes 12582920 | tf_op jit(solution)/shard_map/ppermute | solution.py:20
  13.1 102.3 %copy-start.1 = (s32[8]{0:T(128)S(1)}, s32[8]{0:T(128)}, u32[]{:S(2)}) copy-start(s32[8]{0:T(128)} %param.16) | copy-start | bytes 100
  13.1 102.3 %copy-start.2 = (s32[8,1]{0,1:T(1,128)S(1)}, s32[8,1]{0,1:T(1,128)}, u32[]{:S(2)}) copy-start(s32[8,1]{0,1:T(1,128)} %param.15) | copy-start | bytes 100
  175.8 298.8 %copy-start.3 = (s32[8,1]{0,1:T(1,128)S(1)}, s32[8,1]{0,1:T(1,128)}, u32[]{:S(2)}) copy-start(s32[8,1]{0,1:T(1,128)} %param.20) | copy-start | bytes 100
  175.8 186.9 %all-reduce.2.cloned.1.call-start = ((), (), s32[]{:S(2)}) async-start(), calls=%async_computation.2 | async-start | bytes 524288 | tf_op jit(solution)/shard_map/psum | solution.py:79
  253.8 292.0 %all-gather.4.cloned.1.call-start = ((), (), s32[]{:S(2)}) async-start(), calls=%async_computation.3 | async-start | bytes 8912896 | tf_op jit(solution)/shard_map/all_gather | solution.py:84
  471.2 173.0 %all-gather.6.cloned.1.call-start = ((), (), s32[]{:S(2)}) async-start(), calls=%async_computation.4 | async-start | bytes 17825792 | tf_op jit(solution)/shard_map/all_gather | solution.py:82
  668.8 4.5 collective-permute-start.2
  686.6 6.1 collective-permute-start.3
  706.0 4.4 collective-permute-start.4
  723.7 5.9 collective-permute-start.5
Sparse Core Ops, SparseCore 0:
  175.9 74.8 reduce-scatter.1
  253.9 108.7 all-reduce.1
  471.3 74.4 all-gather.3
  547.5 96.6 all-gather.5
